TPU v7x, 256 devices: a whole 4x4x8 slice. The times are simulated.
256 devices in a mesh: seq: 64 (over x, z_lo, y, core), tensor: 4 (over z_hi).
Axes of the slice: x: 4, y: 4, z: 8 (z_hi: 4, z_lo: 2; z = z_hi * 2 + z_lo), core: 2. Of those that a mesh axis runs over, the one named last changes fastest.
Arguments:
- q_tok: bfloat16 [32768, 1536], P('seq', 'tensor'), may hold values from -24 to 24
- k_tok: bfloat16 [32768, 1536], P('seq', 'tensor'), may hold values from -6 to 6
- v_tok: bfloat16 [32768, 1536], P('seq', 'tensor'), may hold values from -16 to 16
- ref_hidden: bfloat16 [2048, 3072], P('seq', 'tensor'), may hold values from -16 to 16
- ref_wk: bfloat16 [3072, 1536], P('tensor'), may hold values from -0.109375 to 0.109375
- ref_wv: bfloat16 [3072, 1536], P('tensor'), may hold values from -0.109375 to 0.109375
- key_gain: float32 [128], replicated, may hold values from 1 to 2
Outputs:
- attended: bfloat16 [32768, 1536], P('seq', 'tensor')
All inputs are finite; a program needn't handle non-finite values.
Results may differ from a plain program's by a relative error of at most 0.022.
Values may be sent and summed in bfloat16 or wider, within the bound.
No kernel may reach another device: no remote copies, remote signals or barrier semaphores. Data moves between devices by JAX's collectives and lax.ppermute only.
A program may use at most 128 MiB of HBM per device.

v0:
```python
import jax
import jax.numpy as jnp
from jax import lax
from jax.sharding import PartitionSpec as P

HD = 128
VIEW_LEN = 4096
EPSILON = 1e-06


def from_partner(block, axis, apart):
    count = lax.axis_size(axis)
    route = []
    for low in range(count):
        high = low | 1 << apart
        if high != low and high < count:
            route += [(low, high), (high, low)]
    return lax.ppermute(block, axis, route)


def attend(carried, queries, key_rows, values):
    running_max, running_sum, weighted = carried
    head_count = queries.shape[1] // HD
    factor = HD ** (-0.5)
    new_maxes, new_sums, new_weighted = ([], [], [])
    for head_index in range(head_count):
        col_start = head_index * HD
        col_stop = col_start + HD
        scores = (
            jnp.einsum(
                "qd,kd->qk",
                queries[:, col_start:col_stop],
                key_rows[:, col_start:col_stop],
                preferred_element_type=jnp.float32,
            )
            * factor
        )
        raised = jnp.maximum(running_max[head_index], jnp.max(scores, axis=1))
        rescale = jnp.exp(running_max[head_index] - raised)
        weights = jnp.exp(scores - raised[:, None])
        new_sums.append(running_sum[head_index] * rescale + jnp.sum(weights, axis=1))
        product = jnp.dot(
            weights.astype(jnp.bfloat16),
            values[:, col_start:col_stop],
            preferred_element_type=jnp.float32,
        )
        new_weighted.append(weighted[:, col_start:col_stop] * rescale[:, None] + product)
        new_maxes.append(raised)
    return (jnp.stack(new_maxes), jnp.stack(new_sums), jnp.concatenate(new_weighted, axis=1))


def reference_pair(ref_hidden, ref_wk, ref_wv, key_gain):
    k_partial = jnp.dot(ref_hidden, ref_wk, preferred_element_type=jnp.float32)
    v_partial = jnp.dot(ref_hidden, ref_wv, preferred_element_type=jnp.float32)
    row_count = ref_hidden.shape[0]
    groups = lax.axis_size("tensor")
    group_width = k_partial.shape[1] // groups
    stacked = jnp.stack(
        (
            k_partial.reshape(row_count, groups, group_width),
            v_partial.reshape(row_count, groups, group_width),
        ),
        axis=2,
    ).reshape(row_count, 2 * groups * group_width)
    summed = lax.psum_scatter(
        stacked.astype(jnp.bfloat16), "tensor", scatter_dimension=1, tiled=True
    ).astype(jnp.float32)
    raw_keys = summed[:, :group_width].reshape(row_count, group_width // HD, HD)
    normed = (
        raw_keys
        * lax.rsqrt(jnp.mean(raw_keys * raw_keys, axis=2, keepdims=True) + EPSILON)
        * key_gain
    )
    return (
        normed.reshape(row_count, group_width).astype(jnp.bfloat16),
        summed[:, group_width:].astype(jnp.bfloat16),
    )


def per_device(q_tok, k_tok, v_tok, ref_hidden, ref_wk, ref_wv, key_gain):
    ref_keys, ref_vals = reference_pair(ref_hidden, ref_wk, ref_wv, key_gain)
    query_rows = q_tok.shape[0]
    heads_here = q_tok.shape[1] // HD
    group_size = VIEW_LEN // query_rows
    view_bits = group_size.bit_length() - 1
    initial = (
        jnp.full((heads_here, query_rows), -jnp.inf, jnp.float32),
        jnp.zeros((heads_here, query_rows), jnp.float32),
        jnp.zeros(q_tok.shape, jnp.float32),
    )
    view_keys, view_vals = (k_tok, v_tok)
    for bit_index in range(view_bits):
        other_keys, other_vals = from_partner((view_keys, view_vals), "seq", bit_index)
        view_keys = jnp.concatenate((view_keys, other_keys), axis=0)
        view_vals = jnp.concatenate((view_vals, other_vals), axis=0)
    carried = attend(initial, q_tok, view_keys, view_vals)
    carried = attend(
        carried,
        q_tok,
        lax.all_gather(ref_keys, "seq", axis=0, tiled=True),
        lax.all_gather(ref_vals, "seq", axis=0, tiled=True),
    )
    running_max, running_sum, weighted = carried
    spread = jnp.repeat(running_sum.T, HD, axis=1)
    return (weighted / spread).astype(jnp.bfloat16)


def solution(mesh):
    placed = (
        P("seq", "tensor"),
        P("seq", "tensor"),
        P("seq", "tensor"),
        P("seq", "tensor"),
        P("tensor", None),
        P("tensor", None),
        P(),
    )
    return jax.shard_map(
        per_device, mesh=mesh, in_specs=placed, out_specs=P("seq", "tensor"), check_vma=False
    )
```

profile of v0, /device:TPU:1, one launch (start us, length us, event | category | flops | bytes accessed | tf_op | source)
XLA Modules:
  0.0 341.4 jit_solution(11778259846070906958)
XLA Ops:
  6.6 1.6 copy-done
  8.2 1.3 convolution_convert_fusion.1
  9.6 2.2 convolution_convert_fusion
  13.2 27.0 %reduce-scatter.2.cloned.1.call-done = bf16[32,768]{1,0:T(8,128)(2,1)} async-done(((bf16[32,3072]{1,0:T(8,128)(2,1)}), bf16[32,768]{1,0:T(8,128)(2,1)}) %reduce-scatter.2.cloned.1.call-update) | async-done | bytes 49168 | tf_op jit(solution)/shard_map/reduce_scatter | solution.py:65
  41.3 1.4 fusion.83
  42.7 3.0 collective-permute-start
  45.7 1.3 collective-permute-done
  47.1 1.3 collective-permute-start.1
  49.1 16.9 %collective-permute-done.1 = bf16[1024,384]{1,0:T(8,128)(2,1)S(1)} collective-permute-done((bf16[1024,384]{1,0:T(8,128)(2,1)S(1)}, bf16[1024,384]{1,0:T(8,128)(2,1)S(1)}, u32[]{:S(2)}, u32[]{:S(2)}) %collective-permute-start.1) | collective-permute-done | bytes 786464 | tf_op jit(solution)/shard_map/ppermute | solution.py:18
  66.0 1.3 pad_maximum_fusion
  67.3 3.8 %collective-permute-start.2 = (bf16[2048,384]{1,0:T(8,128)(2,1)}, bf16[2048,384]{1,0:T(8,128)(2,1)}, u32[]{:S(2)}, u32[]{:S(2)}) collective-permute-start(bf16[2048,384]{1,0:T(8,128)(2,1)} %pad_maximum_fusion), channel_id=1, source_target_pairs={{0,16},{16,0},{4,20},{20,4},{8,24},{24,8},{12,28},{28,12},{32,48},... | collective-permute-start | bytes 4718600 | tf_op jit(solution)/shard_map/ppermute | solution.py:18
  71.1 1.0 pad_maximum_fusion.3
  76.2 45.3 %collective-permute-done.4 = bf16[1024,384]{1,0:T(8,128)(2,1)S(1)} collective-permute-done((bf16[1024,384]{1,0:T(8,128)(2,1)}, bf16[1024,384]{1,0:T(8,128)(2,1)S(1)}, u32[]{:S(2)}, u32[]{:S(2)}) %collective-permute-start.4) | collective-permute-done | bytes 786464 | tf_op jit(solution)/shard_map/ppermute | solution.py:18
  121.7 3.4 collective-permute-start.5
  125.1 1.0 constant_dynamic-update-slice_fusion.1
  127.0 2.7 constant_dynamic-update-slice_fusion
  129.7 2.6 multiply_reduce_fusion
  132.4 1.3 multiply_reduce_fusion.1
  133.7 1.3 multiply_reduce_fusion.2
  135.6 1.5 fusion.4
  137.1 1.1 copy-done.3
  138.2 1.5 fusion.2
  139.6 18.5 %collective-permute-done.5 = bf16[2048,384]{1,0:T(8,128)(2,1)S(1)} collective-permute-done((bf16[2048,384]{1,0:T(8,128)(2,1)S(1)}, bf16[2048,384]{1,0:T(8,128)(2,1)S(1)}, u32[]{:S(2)}, u32[]{:S(2)}) %collective-permute-start.5) | collective-permute-done | bytes 1572896 | tf_op jit(solution)/shard_map/ppermute | solution.py:18
  158.4 1.6 copy-done.17
  160.0 1.4 fusion
  161.5 50.6 %all-gather.3.cloned.1.call-done = bf16[2048,384]{1,0:T(8,128)(2,1)} async-done(((bf16[32,384]{1,0:T(8,128)(2,1)}), bf16[2048,384]{1,0:T(8,128)(2,1)}) %all-gather.3.cloned.1.call-update) | async-done | bytes 1572880 | tf_op jit(solution)/shard_map/all_gather | solution.py:100
  212.1 1.9 multiply_reduce_fusion.3
  219.2 98.7 %all-gather.5.cloned.1.call-done = bf16[2048,384]{1,0:T(8,128)(2,1)} async-done(((bf16[32,384]{1,0:T(8,128)(2,1)}), bf16[2048,384]{1,0:T(8,128)(2,1)}) %all-gather.5.cloned.1.call-update) | async-done | bytes 1572880 | tf_op jit(solution)/shard_map/all_gather | solution.py:101
  318.0 3.3 fusion.18
  321.3 5.3 %fusion.54 = f32[512,128]{0,1:T(8,128)S(1)} fusion(f32[512,128]{0,1:T(8,128)S(1)} %fusion.18, f32[4096,512]{1,0:T(8,128)} %copy-done.4, f32[512]{0:T(512)S(1)} %get-tuple-element.14, bf16[4096,384]{1,0:T(8,128)(2,1)} %copy-done.17, f32[512]{0:T(512)S(1)} %get-tuple-element.9, f32[512]{0:T(512)S(1)} %get-tuple-element.13), kind=kOutput, calls=%fused_computation.48 | convolution fusion | flops 543358976 | bytes 9967616 | tf_op jit(solution)/shard_map/dot_general | solution.py:42
  328.5 1.6 fusion.45
  332.2 1.6 fusion.36
  (93 shorter events, 19.8 us)
Async XLA Ops:
  6.5 6.6 %copy-start.19 = (f32[128]{0:T(128)S(1)}, f32[128]{0:T(128)}, u32[]{:S(2)}) copy-start(f32[128]{0:T(128)} %param.13) | copy-start | bytes 1540
  6.5 36.2 %copy-start.11 = (bf16[512,384]{1,0:T(8,128)(2,1)S(1)}, bf16[512,384]{1,0:T(8,128)(2,1)}, u32[]{:S(2)}) copy-start(bf16[512,384]{1,0:T(8,128)(2,1)} %param.8) | copy-start | bytes 1179652
  6.5 41.9 %copy-start.12 = (bf16[512,384]{1,0:T(8,128)(2,1)S(1)}, bf16[512,384]{1,0:T(8,128)(2,1)}, u32[]{:S(2)}) copy-start(bf16[512,384]{1,0:T(8,128)(2,1)} %param.9) | copy-start | bytes 1179652
  6.5 33.7 %reduce-scatter.2.cloned.1.call-start = ((), (), s32[]{:S(2)}) async-start(), calls=%async_computation.1 | async-start | bytes 245760 | tf_op jit(solution)/shard_map/reduce_scatter | solution.py:65
  13.1 199.0 %all-gather.3.cloned.1.call-start = ((), (), s32[]{:S(2)}) async-start(), calls=%async_computation.2 | async-start | bytes 1597440 | tf_op jit(solution)/shard_map/all_gather | solution.py:100
  40.2 33.8 %copy-start.15 = (bf16[32,768]{1,0:T(8,128)(2,1)S(1)}, bf16[32,768]{1,0:T(8,128)(2,1)}, u32[]{:S(2)}) copy-start(bf16[32,768]{1,0:T(8,128)(2,1)} %reduce-scatter.2.cloned.1.call-done) | copy-start | bytes 147460
  42.7 275.3 %all-gather.5.cloned.1.call-start = ((), (), s32[]{:S(2)}) async-start(), calls=%async_computation.3 | async-start | bytes 1597440 | tf_op jit(solution)/shard_map/all_gather | solution.py:101
  42.7 4.3 %collective-permute-start = (bf16[512,384]{1,0:T(8,128)(2,1)S(1)}, bf16[512,384]{1,0:T(8,128)(2,1)S(1)}, u32[]{:S(2)}, u32[]{:S(2)}) collective-permute-start(bf16[512,384]{1,0:T(8,128)(2,1)S(1)} %copy-done.11), channel_id=1, source_target_pairs={{0,4},{4,0},{8,12},{12,8},{16,20},{20,16},{24,28},{28,24},{32,36},... | collective-permute-start | bytes 1179656 | tf_op jit(solution)/shard_map/ppermute | solution.py:18
  47.1 18.8 %collective-permute-start.1 = (bf16[1024,384]{1,0:T(8,128)(2,1)S(1)}, bf16[1024,384]{1,0:T(8,128)(2,1)S(1)}, u32[]{:S(2)}, u32[]{:S(2)}) collective-permute-start(bf16[1024,384]{1,0:T(8,128)(2,1)S(1)} %pad_maximum_fusion.2), channel_id=1, source_target_pairs={{0,8},{8,0},{4,12},{12,4},{16,24},{24,16},{20,28},{28,20},{32,40},... | collective-permute-start | bytes 2359304 | tf_op jit(solution)/shard_map/ppermute | solution.py:18
  48.4 22.6 %collective-permute-start.3 = (bf16[512,384]{1,0:T(8,128)(2,1)S(1)}, bf16[512,384]{1,0:T(8,128)(2,1)S(1)}, u32[]{:S(2)}, u32[]{:S(2)}) collective-permute-start(bf16[512,384]{1,0:T(8,128)(2,1)S(1)} %copy-done.12), channel_id=1, source_target_pairs={{0,4},{4,0},{8,12},{12,8},{16,20},{20,16},{24,28},{28,24},{32,36},... | collective-permute-start | bytes 1179656 | tf_op jit(solution)/shard_map/ppermute | solution.py:18
  67.3 59.7 %collective-permute-start.2 = (bf16[2048,384]{1,0:T(8,128)(2,1)}, bf16[2048,384]{1,0:T(8,128)(2,1)}, u32[]{:S(2)}, u32[]{:S(2)}) collective-permute-start(bf16[2048,384]{1,0:T(8,128)(2,1)} %pad_maximum_fusion), channel_id=1, source_target_pairs={{0,16},{16,0},{4,20},{20,4},{8,24},{24,8},{12,28},{28,12},{32,48},... | collective-permute-start | bytes 4718600 | tf_op jit(solution)/shard_map/ppermute | solution.py:18
  72.1 49.4 %collective-permute-start.4 = (bf16[1024,384]{1,0:T(8,128)(2,1)}, bf16[1024,384]{1,0:T(8,128)(2,1)S(1)}, u32[]{:S(2)}, u32[]{:S(2)}) collective-permute-start(bf16[1024,384]{1,0:T(8,128)(2,1)} %pad_maximum_fusion.3), channel_id=1, source_target_pairs={{0,8},{8,0},{4,12},{12,4},{16,24},{24,16},{20,28},{28,20},{32,40},... | collective-permute-start | bytes 2359304 | tf_op jit(solution)/shard_map/ppermute | solution.py:18
  76.2 53.5 %copy-start.13 = (bf16[512,384]{1,0:T(8,128)(2,1)S(1)}, bf16[512,384]{1,0:T(8,128)(2,1)}, u32[]{:S(2)}) copy-start(bf16[512,384]{1,0:T(8,128)(2,1)} %param.7) | copy-start | bytes 1179652
  121.7 36.4 %collective-permute-start.5 = (bf16[2048,384]{1,0:T(8,128)(2,1)S(1)}, bf16[2048,384]{1,0:T(8,128)(2,1)S(1)}, u32[]{:S(2)}, u32[]{:S(2)}) collective-permute-start(bf16[2048,384]{1,0:T(8,128)(2,1)S(1)} %pad_maximum_fusion.1), channel_id=1, source_target_pairs={{0,16},{16,0},{4,20},{20,4},{8,24},{24,8},{12,28},{28,12},{32,48},... | collective-permute-start | bytes 4718600 | tf_op jit(solution)/shard_map/ppermute | solution.py:18
  129.7 2.6 copy-start.10
  132.4 3.2 copy-start.4
  133.7 4.5 %copy-start.3 = (f32[4096,512]{1,0:T(8,128)}, f32[4096,512]{1,0:T(8,128)S(1)}, u32[]{:S(2)}) copy-start(f32[4096,512]{1,0:T(8,128)S(1)} %get-tuple-element.19) | copy-start | bytes 25165828
  134.9 25.1 %copy-start.2 = (f32[4096,512]{1,0:T(8,128)}, f32[4096,512]{1,0:T(8,128)S(1)}, u32[]{:S(2)}) copy-start(f32[4096,512]{1,0:T(8,128)S(1)} %get-tuple-element.23) | copy-start | bytes 25165828
  138.2 19.9 %copy-start.16 = (bf16[4096,384]{1,0:T(8,128)(2,1)S(1)}, bf16[4096,384]{1,0:T(8,128)(2,1)}, u32[]{:S(2)}) copy-start(bf16[4096,384]{1,0:T(8,128)(2,1)} %constant_dynamic-update-slice_fusion.5) | copy-start | bytes 9437188
  212.1 1.9 copy-start.14
  214.0 2.1 copy-start.9
  214.7 2.4 copy-start.7
  215.5 3.0 copy-start.5
  317.9 8.7 %copy-start.20 = (bf16[2048,384]{1,0:T(8,128)(2,1)S(1)}, bf16[2048,384]{1,0:T(8,128)(2,1)}, u32[]{:S(2)}) copy-start(bf16[2048,384]{1,0:T(8,128)(2,1)} %all-gather.5.cloned.1.call-done) | copy-start | bytes 4718596
  318.0 9.6 %slice-start.2 = ((s8[8388608]{0:T(1024)(128)(4,1)}), s8[4194304]{0:T(1024)(128)(4,1)S(1)}, s32[]{:S(2)}) async-start(s8[8388608]{0:T(1024)(128)(4,1)} %bitcast.27), calls=%async_computation.6 | async-start | bytes 8388608
  321.3 5.4 %copy-start.8 = (f32[2048,512]{1,0:T(8,128)S(1)}, f32[2048,512]{1,0:T(8,128)}, u32[]{:S(2)}) copy-start(f32[2048,512]{1,0:T(8,128)} %copy-done.7) | copy-start | bytes 12582916
  321.3 6.3 %slice-start.3 = ((s8[8388608]{0:T(1024)(128)(4,1)}), s8[4194304]{0:T(1024)(128)(4,1)S(1)}, s32[]{:S(2)}) async-start(s8[8388608]{0:T(1024)(128)(4,1)} %bitcast.27), calls=%async_computation.7 | async-start | bytes 8388608
  321.3 7.2 %copy-start.18 = (bf16[4096,384]{1,0:T(8,128)(2,1)S(1)}, bf16[4096,384]{1,0:T(8,128)(2,1)}, u32[]{:S(2)}) copy-start(bf16[4096,384]{1,0:T(8,128)(2,1)} %copy-done.17) | copy-start | bytes 9437188
  326.7 5.0 %slice-start = ((s8[8388608]{0:T(1024)(128)(4,1)}), s8[4194304]{0:T(1024)(128)(4,1)S(1)}, s32[]{:S(2)}) async-start(s8[8388608]{0:T(1024)(128)(4,1)} %bitcast.25), calls=%async_computation.4 | async-start | bytes 8388608
  328.5 2.2 copy-start.6
  328.5 3.7 %slice-start.1 = ((s8[8388608]{0:T(1024)(128)(4,1)}), s8[4194304]{0:T(1024)(128)(4,1)S(1)}, s32[]{:S(2)}) async-start(s8[8388608]{0:T(1024)(128)(4,1)} %bitcast.25), calls=%async_computation.5 | async-start | bytes 8388608
  331.6 3.3 copy-start.1
  (2 other events, 3.3 us)
Sparse Core Ops, SparseCore 0:
  13.2 26.9 reduce-scatter.1
  42.8 169.2 all-gather.2
  214.1 103.7 all-gather.4
where the time goes:
time: 342 us; the launch traced here: 341 us
  waiting for transfers between devices  258 us (75%)
  matrix products  25.5 us (7%)
  local copies, waits for them, and re-layouts  19.2 us (6%)
  between operations  13.5 us (4%)
  starting transfers between devices  12.5 us (4%)
  other arithmetic  12.3 us (4%)
    all_gather x1, waiting for transfers between devices, per_device(): lax.all_gather(ref_vals, 'seq', axis=0, tiled=True)  98.7 us
    ppermute x6, waiting for transfers between devices, from_partner(): return lax.ppermute(block, axis, route)  82 us
    all_gather x1, waiting for transfers between devices, per_device(): lax.all_gather(ref_keys, 'seq', axis=0, tiled=True)  50.6 us
    reduce_scatter x1, waiting for transfers between devices, reference_pair(): lax.psum_scatter(stacked.astype(jnp.bfloat16), 'tensor', scatter_dimensio...  27 us
    dot_general x6, matrix products, attend(): jnp.dot(weights.astype(jnp.bfloat16), values[:, col_start:col_stop], pref...  13.6 us
    unnamed x56, local copies, waits for them, and re-layouts  13.5 us
    ppermute x6, starting transfers between devices, from_partner(): return lax.ppermute(block, axis, route)  12.4 us
    dot_general x6, matrix products, attend(): jnp.einsum('qd,kd->qk', queries[:, col_start:col_stop], key_rows[:, col_s...  8.46 us
  transfers between devices with their start and end apart: 9, of which 7 were waited for; matrix products, arithmetic and copies ran while one was open for 8% of the time, Pallas kernels for 0%

commit v1 on v0

--- a/solution.py
+++ b/solution.py
@@ -97,7 +97,9 @@
     carried = attend(
         carried,
         q_tok,
-        lax.all_gather(ref_keys, "seq", axis=0, tiled=True),
+        jnp.concatenate(
+            lax.all_to_all(jnp.stack([ref_keys] * lax.axis_size("seq")), "seq", 0, 0), axis=0
+        ),
         lax.all_gather(ref_vals, "seq", axis=0, tiled=True),
     )
     running_max, running_sum, weighted = carried

time: 342 us -> 247 us (0.72)
  waiting for transfers between devices: 258 us -> 151 us
  local copies, waits for them, and re-layouts: 19.2 us -> 24.5 us
  other arithmetic: 12.3 us -> 16.9 us
  starting transfers between devices: 12.5 us -> 16.4 us
    all_gather x1 -> x0, waiting for transfers between devices: 50.6 us -> none  [per_device(): lax.all_gather(ref_keys, 'seq', axis=0, tiled=True)]
    all_gather x1, waiting for transfers between devices: 98.7 us -> 69.5 us  [per_device(): lax.all_gather(ref_vals, 'seq', axis=0, tiled=True)]
    reduce_scatter x1, waiting for transfers between devices: 27 us -> 0.01 us  [reference_pair(): lax.psum_scatter(stacked.astype(jnp.bfloat16), 'tensor', scatter_dimensio...]
    all_to_all x0 -> x1, starting transfers between devices: none -> 9.06 us  [per_device(): lax.all_to_all(jnp.stack([ref_keys] * lax.axis_size('seq')), 'seq', 0, 0)]
    ppermute x6, starting transfers between devices: 12.4 us -> 7.3 us  [from_partner(): return lax.ppermute(block, axis, route)]
    unnamed x56 -> x48, local copies, waits for them, and re-layouts: 13.5 us -> 13.5 us
  transfers between devices with their start and end apart: 9 -> 9, of which waited for: 7 -> 6; matrix products, arithmetic and copies ran while one was open for 8% -> 18% of each run, Pallas kernels for 0% -> 0%
where the time goes in v1:
time: 247 us; the launch traced here: 246 us
  waiting for transfers between devices  151 us (61%)
  local copies, waits for them, and re-layouts  24.5 us (10%)
  matrix products  23.6 us (10%)
  other arithmetic  16.9 us (7%)
  starting transfers between devices  16.4 us (7%)
  between operations  13.7 us (6%)
    ppermute x6, waiting for transfers between devices, from_partner(): return lax.ppermute(block, axis, route)  81.1 us
    all_gather x1, waiting for transfers between devices, per_device(): lax.all_gather(ref_vals, 'seq', axis=0, tiled=True)  69.5 us
    dot_general x6, matrix products, attend(): jnp.dot(weights.astype(jnp.bfloat16), values[:, col_start:col_stop], pref...  13.5 us
    unnamed x48, local copies, waits for them, and re-layouts  13.5 us
    all_to_all x1, starting transfers between devices, per_device(): lax.all_to_all(jnp.stack([ref_keys] * lax.axis_size('seq')), 'seq', 0, 0)  9.06 us
    ppermute x6, starting transfers between devices, from_partner(): return lax.ppermute(block, axis, route)  7.3 us
    reduce_sum x6, other arithmetic, attend(): jnp.sum(weights, axis=1)  6.84 us
    dot_general x6, matrix products, attend(): jnp.einsum('qd,kd->qk', queries[:, col_start:col_stop], key_rows[:, col_s...  5.92 us
  transfers between devices with their start and end apart: 9, of which 6 were waited for; matrix products, arithmetic and copies ran while one was open for 18% of the time, Pallas kernels for 0%

profile of v1, /device:TPU:1, one launch (start us, length us, event | category | flops | bytes accessed | tf_op | source)
XLA Modules:
  0.0 245.8 jit_solution(14278400234809139942)
XLA Ops:
  6.5 3.2 %collective-permute-start = (bf16[512,384]{1,0:T(8,128)(2,1)}, bf16[512,384]{1,0:T(8,128)(2,1)S(1)}, u32[]{:S(2)}, u32[]{:S(2)}) collective-permute-start(bf16[512,384]{1,0:T(8,128)(2,1)} %param.8), channel_id=1, source_target_pairs={{0,4},{4,0},{8,12},{12,8},{16,20},{20,16},{24,28},{28,24},{32,36},... | collective-permute-start | bytes 1179656 | tf_op jit(solution)/shard_map/ppermute | solution.py:18
  9.9 1.5 collective-permute-done
  11.3 2.0 pad_maximum_fusion.2
  13.3 2.0 convolution_convert_fusion.1
  17.4 1.5 collective-permute-start.4
  18.9 2.2 convolution_convert_fusion
  22.5 9.9 %collective-permute-done.1 = bf16[1024,384]{1,0:T(8,128)(2,1)} collective-permute-done((bf16[1024,384]{1,0:T(8,128)(2,1)}, bf16[1024,384]{1,0:T(8,128)(2,1)}, u32[]{:S(2)}, u32[]{:S(2)}) %collective-permute-start.1) | collective-permute-done | bytes 786464 | tf_op jit(solution)/shard_map/ppermute | solution.py:18
  32.4 2.4 pad_maximum_fusion
  34.8 1.2 collective-permute-start.2
  36.0 13.1 %collective-permute-done.4 = bf16[1024,384]{1,0:T(8,128)(2,1)S(1)} collective-permute-done((bf16[1024,384]{1,0:T(8,128)(2,1)S(1)}, bf16[1024,384]{1,0:T(8,128)(2,1)S(1)}, u32[]{:S(2)}, u32[]{:S(2)}) %collective-permute-start.4) | collective-permute-done | bytes 786464 | tf_op jit(solution)/shard_map/ppermute | solution.py:18
  49.1 2.4 pad_maximum_fusion.1
  51.5 1.3 collective-permute-start.5
  54.3 1.3 slice.80
  57.5 1.3 stack.8
  58.8 9.1 %all-to-all-start = ((bf16[64,32,384]{2,1,0:T(8,128)(2,1)}), bf16[64,32,384]{2,1,0:T(8,128)(2,1)S(1)}, u32[]{:S(2)}, u32[]{:S(2)}) async-start(bf16[64,32,384]{2,1,0:T(8,128)(2,1)} %stack.8), calls=%async_computation.1 | async-start | bytes 3145728 | tf_op jit(solution)/shard_map/all_to_all | solution.py:101
  68.7 1.8 constant_dynamic-update-slice_fusion.6
  70.5 2.1 constant_dynamic-update-slice_fusion.1
  73.5 25.7 %collective-permute-done.2 = bf16[2048,384]{1,0:T(8,128)(2,1)} collective-permute-done((bf16[2048,384]{1,0:T(8,128)(2,1)}, bf16[2048,384]{1,0:T(8,128)(2,1)}, u32[]{:S(2)}, u32[]{:S(2)}) %collective-permute-start.2) | collective-permute-done | bytes 1572896 | tf_op jit(solution)/shard_map/ppermute | solution.py:18
  99.2 2.7 %constant_dynamic-update-slice_fusion = bf16[4096,384]{1,0:T(8,128)(2,1)} fusion(bf16[4096,384]{1,0:T(8,128)(2,1)} %constant_dynamic-update-slice_fusion.1, bf16[2048,384]{1,0:T(8,128)(2,1)} %collective-permute-done.2), kind=kLoop, calls=%fused_computation.82 | loop fusion | bytes 3145728 | tf_op jit(solution)/shard_map/concatenate | solution.py:94
  101.9 31.0 %collective-permute-done.5 = bf16[2048,384]{1,0:T(8,128)(2,1)} collective-permute-done((bf16[2048,384]{1,0:T(8,128)(2,1)}, bf16[2048,384]{1,0:T(8,128)(2,1)}, u32[]{:S(2)}, u32[]{:S(2)}) %collective-permute-start.5) | collective-permute-done | bytes 1572896 | tf_op jit(solution)/shard_map/ppermute | solution.py:18
  132.9 2.7 %constant_dynamic-update-slice_fusion.4 = bf16[4096,384]{1,0:T(8,128)(2,1)} fusion(bf16[4096,384]{1,0:T(8,128)(2,1)} %constant_dynamic-update-slice_fusion.5, bf16[2048,384]{1,0:T(8,128)(2,1)} %collective-permute-done.5), kind=kLoop, calls=%fused_computation.86 | loop fusion | bytes 3145728 | tf_op jit(solution)/shard_map/concatenate | solution.py:95
  135.6 1.3 multiply_reduce_fusion
  136.9 1.3 multiply_reduce_fusion.1
  138.2 1.3 multiply_reduce_fusion.2
  140.1 1.5 fusion.4
  142.6 1.5 fusion.2
  145.2 1.4 fusion
  152.6 69.5 %all-gather.2.cloned.1.call-done = bf16[2048,384]{1,0:T(8,128)(2,1)} async-done(((bf16[32,384]{1,0:T(8,128)(2,1)}), bf16[2048,384]{1,0:T(8,128)(2,1)}) %all-gather.2.cloned.1.call-update) | async-done | bytes 1572880 | tf_op jit(solution)/shard_map/all_gather | solution.py:103
  222.0 3.3 %fusion.18 = f32[512,128]{0,1:T(8,128)S(1)} fusion(f32[2048,512]{1,0:T(8,128)} %copy-done.9, f32[512]{0:T(512)S(1)} %get-tuple-element.10, bf16[2048,384]{1,0:T(8,128)(2,1)} %all-gather.2.cloned.1.call-done), kind=kOutput, calls=%fused_computation.29 | convolution fusion | flops 271581184 | bytes 4982784 | tf_op jit(solution)/shard_map/dot_general | solution.py:42
  225.4 5.3 %fusion.54 = f32[512,128]{0,1:T(8,128)S(1)} fusion(f32[512,128]{0,1:T(8,128)S(1)} %fusion.18, f32[4096,512]{1,0:T(8,128)} %copy-done.4, f32[512]{0:T(512)S(1)} %get-tuple-element.14, bf16[4096,384]{1,0:T(8,128)(2,1)} %constant_dynamic-update-slice_fusion.4, f32[512]{0:T(512)S(1)} %get-tuple-element.9, f32[512]{0:T(512)S(1)} %get-tuple-element.13), kind=kOutput, calls=%fused_computation.48 | convolution fusion | flops 543358976 | bytes 9967616 | tf_op jit(solution)/shard_map/dot_general | solution.py:42
  232.6 1.6 fusion.45
  236.3 1.6 fusion.36
  (85 shorter events, 22.3 us)
Async XLA Ops:
  6.5 6.8 %copy-start = (bf16[768,1536]{1,0:T(8,128)(2,1)S(1)}, bf16[768,1536]{1,0:T(8,128)(2,1)}, u32[]{:S(2)}) copy-start(bf16[768,1536]{1,0:T(8,128)(2,1)} %param.11) | copy-start | bytes 7077892
  6.5 9.7 %copy-start.12 = (bf16[512,384]{1,0:T(8,128)(2,1)S(1)}, bf16[512,384]{1,0:T(8,128)(2,1)}, u32[]{:S(2)}) copy-start(bf16[512,384]{1,0:T(8,128)(2,1)} %param.9) | copy-start | bytes 1179652
  6.5 47.8 %reduce-scatter.2.cloned.1.call-start = ((), (), s32[]{:S(2)}) async-start(), calls=%async_computation.2 | async-start | bytes 245760 | tf_op jit(solution)/shard_map/reduce_scatter | solution.py:65
  6.5 4.8 %collective-permute-start = (bf16[512,384]{1,0:T(8,128)(2,1)}, bf16[512,384]{1,0:T(8,128)(2,1)S(1)}, u32[]{:S(2)}, u32[]{:S(2)}) collective-permute-start(bf16[512,384]{1,0:T(8,128)(2,1)} %param.8), channel_id=1, source_target_pairs={{0,4},{4,0},{8,12},{12,8},{16,20},{20,16},{24,28},{28,24},{32,36},... | collective-permute-start | bytes 1179656 | tf_op jit(solution)/shard_map/ppermute | solution.py:18
  9.8 6.5 %collective-permute-start.3 = (bf16[512,384]{1,0:T(8,128)(2,1)}, bf16[512,384]{1,0:T(8,128)(2,1)}, u32[]{:S(2)}, u32[]{:S(2)}) collective-permute-start(bf16[512,384]{1,0:T(8,128)(2,1)} %param.9), channel_id=1, source_target_pairs={{0,4},{4,0},{8,12},{12,8},{16,20},{20,16},{24,28},{28,24},{32,36},... | collective-permute-start | bytes 1179656 | tf_op jit(solution)/shard_map/ppermute | solution.py:18
  13.3 9.2 %copy-start.15 = (f32[128]{0:T(128)S(1)}, f32[128]{0:T(128)}, u32[]{:S(2)}) copy-start(f32[128]{0:T(128)} %param.13) | copy-start | bytes 1540
  13.3 19.1 %copy-start.11 = (bf16[512,384]{1,0:T(8,128)(2,1)S(1)}, bf16[512,384]{1,0:T(8,128)(2,1)}, u32[]{:S(2)}) copy-start(bf16[512,384]{1,0:T(8,128)(2,1)} %param.8) | copy-start | bytes 1179652
  13.3 19.1 %collective-permute-start.1 = (bf16[1024,384]{1,0:T(8,128)(2,1)}, bf16[1024,384]{1,0:T(8,128)(2,1)}, u32[]{:S(2)}, u32[]{:S(2)}) collective-permute-start(bf16[1024,384]{1,0:T(8,128)(2,1)} %pad_maximum_fusion.2), channel_id=1, source_target_pairs={{0,8},{8,0},{4,12},{12,4},{16,24},{24,16},{20,28},{28,20},{32,40},... | collective-permute-start | bytes 2359304 | tf_op jit(solution)/shard_map/ppermute | solution.py:18
  17.4 31.8 %collective-permute-start.4 = (bf16[1024,384]{1,0:T(8,128)(2,1)S(1)}, bf16[1024,384]{1,0:T(8,128)(2,1)S(1)}, u32[]{:S(2)}, u32[]{:S(2)}) collective-permute-start(bf16[1024,384]{1,0:T(8,128)(2,1)S(1)} %pad_maximum_fusion.3), channel_id=1, source_target_pairs={{0,8},{8,0},{4,12},{12,4},{16,24},{24,16},{20,28},{28,20},{32,40},... | collective-permute-start | bytes 2359304 | tf_op jit(solution)/shard_map/ppermute | solution.py:18
  22.4 199.6 %all-gather.2.cloned.1.call-start = ((), (), s32[]{:S(2)}) async-start(), calls=%async_computation.3 | async-start | bytes 1597440 | tf_op jit(solution)/shard_map/all_gather | solution.py:103
  34.8 64.4 %collective-permute-start.2 = (bf16[2048,384]{1,0:T(8,128)(2,1)}, bf16[2048,384]{1,0:T(8,128)(2,1)}, u32[]{:S(2)}, u32[]{:S(2)}) collective-permute-start(bf16[2048,384]{1,0:T(8,128)(2,1)} %pad_maximum_fusion), channel_id=1, source_target_pairs={{0,16},{16,0},{4,20},{20,4},{8,24},{24,8},{12,28},{28,12},{32,48},... | collective-permute-start | bytes 4718600 | tf_op jit(solution)/shard_map/ppermute | solution.py:18
  51.5 81.4 %collective-permute-start.5 = (bf16[2048,384]{1,0:T(8,128)(2,1)}, bf16[2048,384]{1,0:T(8,128)(2,1)}, u32[]{:S(2)}, u32[]{:S(2)}) collective-permute-start(bf16[2048,384]{1,0:T(8,128)(2,1)} %pad_maximum_fusion.1), channel_id=1, source_target_pairs={{0,16},{16,0},{4,20},{20,4},{8,24},{24,8},{12,28},{28,12},{32,48},... | collective-permute-start | bytes 4718600 | tf_op jit(solution)/shard_map/ppermute | solution.py:18
  58.8 87.8 %all-to-all-start = ((bf16[64,32,384]{2,1,0:T(8,128)(2,1)}), bf16[64,32,384]{2,1,0:T(8,128)(2,1)S(1)}, u32[]{:S(2)}, u32[]{:S(2)}) async-start(bf16[64,32,384]{2,1,0:T(8,128)(2,1)} %stack.8), calls=%async_computation.1 | async-start | bytes 3145728 | tf_op jit(solution)/shard_map/all_to_all | solution.py:101
  72.6 63.1 %copy-start.13 = (bf16[512,384]{1,0:T(8,128)(2,1)S(1)}, bf16[512,384]{1,0:T(8,128)(2,1)}, u32[]{:S(2)}) copy-start(bf16[512,384]{1,0:T(8,128)(2,1)} %param.7) | copy-start | bytes 1179652
  101.9 33.7 %copy-start.10 = (bf16[4096,384]{1,0:T(8,128)(2,1)S(1)}, bf16[4096,384]{1,0:T(8,128)(2,1)}, u32[]{:S(2)}) copy-start(bf16[4096,384]{1,0:T(8,128)(2,1)} %constant_dynamic-update-slice_fusion) | copy-start | bytes 9437188
  136.9 3.2 %copy-start.4 = (f32[4096,512]{1,0:T(8,128)}, f32[4096,512]{1,0:T(8,128)S(1)}, u32[]{:S(2)}) copy-start(f32[4096,512]{1,0:T(8,128)S(1)} %get-tuple-element.15) | copy-start | bytes 25165828
  138.2 4.5 %copy-start.3 = (f32[4096,512]{1,0:T(8,128)}, f32[4096,512]{1,0:T(8,128)S(1)}, u32[]{:S(2)}) copy-start(f32[4096,512]{1,0:T(8,128)S(1)} %get-tuple-element.19) | copy-start | bytes 25165828
  139.4 5.7 %copy-start.2 = (f32[4096,512]{1,0:T(8,128)}, f32[4096,512]{1,0:T(8,128)S(1)}, u32[]{:S(2)}) copy-start(f32[4096,512]{1,0:T(8,128)S(1)} %get-tuple-element.23) | copy-start | bytes 25165828
  147.3 2.1 copy-start.9
  148.1 2.5 copy-start.7
  148.8 3.0 %copy-start.5 = (f32[2048,512]{1,0:T(8,128)}, f32[2048,512]{1,0:T(8,128)S(1)}, u32[]{:S(2)}) copy-start(f32[2048,512]{1,0:T(8,128)S(1)} %get-tuple-element.25) | copy-start | bytes 12582916
  222.0 8.7 %copy-start.16 = (bf16[2048,384]{1,0:T(8,128)(2,1)S(1)}, bf16[2048,384]{1,0:T(8,128)(2,1)}, u32[]{:S(2)}) copy-start(bf16[2048,384]{1,0:T(8,128)(2,1)} %all-gather.2.cloned.1.call-done) | copy-start | bytes 4718596
  222.0 9.6 %slice-start.2 = ((s8[8388608]{0:T(1024)(128)(4,1)}), s8[4194304]{0:T(1024)(128)(4,1)S(1)}, s32[]{:S(2)}) async-start(s8[8388608]{0:T(1024)(128)(4,1)} %bitcast.28), calls=%async_computation.6 | async-start | bytes 8388608
  225.4 5.4 %copy-start.8 = (f32[2048,512]{1,0:T(8,128)S(1)}, f32[2048,512]{1,0:T(8,128)}, u32[]{:S(2)}) copy-start(f32[2048,512]{1,0:T(8,128)} %copy-done.7) | copy-start | bytes 12582916
  225.4 6.3 %slice-start.3 = ((s8[8388608]{0:T(1024)(128)(4,1)}), s8[4194304]{0:T(1024)(128)(4,1)S(1)}, s32[]{:S(2)}) async-start(s8[8388608]{0:T(1024)(128)(4,1)} %bitcast.28), calls=%async_computation.7 | async-start | bytes 8388608
  225.4 7.2 %copy-start.14 = (bf16[4096,384]{1,0:T(8,128)(2,1)S(1)}, bf16[4096,384]{1,0:T(8,128)(2,1)}, u32[]{:S(2)}) copy-start(bf16[4096,384]{1,0:T(8,128)(2,1)} %constant_dynamic-update-slice_fusion.4) | copy-start | bytes 9437188
  230.7 4.9 %slice-start = ((s8[8388608]{0:T(1024)(128)(4,1)}), s8[4194304]{0:T(1024)(128)(4,1)S(1)}, s32[]{:S(2)}) async-start(s8[8388608]{0:T(1024)(128)(4,1)} %bitcast.26), calls=%async_computation.4 | async-start | bytes 8388608
  232.6 2.2 copy-start.6
  232.6 3.7 %slice-start.1 = ((s8[8388608]{0:T(1024)(128)(4,1)}), s8[4194304]{0:T(1024)(128)(4,1)S(1)}, s32[]{:S(2)}) async-start(s8[8388608]{0:T(1024)(128)(4,1)} %bitcast.26), calls=%async_computation.5 | async-start | bytes 8388608
  235.7 3.3 %copy-start.1 = (bf16[768,1536]{1,0:T(8,128)(2,1)S(1)}, bf16[768,1536]{1,0:T(8,128)(2,1)}, u32[]{:S(2)}) copy-start(bf16[768,1536]{1,0:T(8,128)(2,1)} %param.11) | copy-start | bytes 7077892
Sparse Core Ops, SparseCore 0:
  22.5 24.6 reduce-scatter.1
  55.8 166.1 all-gather.1
